TPU v7x, 128 devices: a whole 4x4x4 slice. The times are simulated.
128 devices in a mesh: band: 4 (over y), dom: 32 (over x, z, core).
Axes of the slice: x: 4, y: 4, z: 4, core: 2. Of those that a mesh axis runs over, the one named last changes fastest.
Arguments:
- orbitals: float32 [1024, 131072], P('band', 'dom'), may hold values from -6 to 6
- projectors: float32 [1024, 512, 128], P('dom'), may hold values from -0.25 to 0.25
- window_start: int32 [1024], P('dom'), may hold values from 0 to 3584
- slot_atom: int32 [32, 32], replicated, may hold values from 0 to 95, as said below
- atom_home: int32 [96], replicated, may hold values from 0 to 95, as said below
- atom_matrices: float32 [96, 128, 128], P('dom'), may hold values from -0.1875 to 0.1875
- rotation: float32 [1024, 1024], P('band'), may hold values from -0.1875 to 0.1875
Outputs:
- rotated: float32 [1024, 131072], P('band', 'dom')
Inputs may be any that keep to these rules, and one draw needn't show every extreme that they name: `atom_home`: a permutation; atom a is owned by domain atom_home[a] // 3, so every domain owns 3 atoms. `slot_atom`: in one domain at most 2 windows have atoms of one owner; in every domain some owner has exactly 2 of them, and some owner has exactly 2 from every domain.
All inputs are finite; a program needn't handle non-finite values.
Results may differ from a plain program's by a relative error of at most 0.0003.
Values sent between devices are 32-bit elements; how exact they have to be, the bound alone decides.
A program may use at most 128 MiB of HBM per device.

v0:
```python
import jax
import jax.numpy as jnp
from jax import lax
from jax.sharding import PartitionSpec as P

HIGHEST = lax.Precision.HIGHEST


def per_device(orbitals, projectors, window_start, slot_atom, atom_home, atom_matrices, rotation):
    own_domain = lax.axis_index("dom")
    slot_count = projectors.shape[0]
    window = projectors.shape[1]
    atom_count = atom_home.shape[0]
    windows = jax.vmap(lambda offset: lax.dynamic_slice_in_dim(orbitals, offset, window, 1))(
        window_start
    )
    partials = jnp.einsum("sbw,swp->sbp", windows, projectors, precision=HIGHEST)
    atom_ids = jnp.arange(atom_count, dtype=jnp.int32)
    home_table = jnp.sum(
        jnp.where(slot_atom[:, :, None] == atom_ids[None, None, :], atom_home[None, None, :], 0),
        axis=2,
    )
    own_home = lax.dynamic_index_in_dim(home_table, own_domain, 0, keepdims=False)
    home_match = (atom_ids[:, None] == own_home[None, :]).astype(jnp.float32)
    per_atom = jnp.einsum("rs,sbp->rbp", home_match, partials, precision=HIGHEST)
    owned_sums = lax.psum_scatter(per_atom, "dom", scatter_dimension=0, tiled=True)
    owned_factors = jnp.einsum("abp,apq->abq", owned_sums, atom_matrices, precision=HIGHEST)
    all_factors = lax.all_gather(owned_factors, "dom", axis=0, tiled=True)
    slot_factors = jnp.einsum("rs,rbp->sbp", home_match, all_factors, precision=HIGHEST)
    updates = jnp.einsum("sbq,swq->sbw", slot_factors, projectors, precision=HIGHEST)

    def add_window(slot_index, current):
        offset = window_start[slot_index]
        previous = lax.dynamic_slice_in_dim(current, offset, window, 1)
        return lax.dynamic_update_slice_in_dim(current, previous + updates[slot_index], offset, 1)

    corrected = lax.fori_loop(0, slot_count, add_window, orbitals)
    return jnp.dot(
        rotation,
        lax.all_gather(corrected, "band", axis=0, tiled=True),
        precision=HIGHEST,
        preferred_element_type=jnp.float32,
    )


def solution(mesh):
    in_specs = (
        P("band", "dom"),
        P("dom", None, None),
        P("dom"),
        P(),
        P(),
        P("dom", None, None),
        P("band", None),
    )
    out_specs = P("band", "dom")
    return jax.shard_map(
        per_device, mesh=mesh, in_specs=in_specs, out_specs=out_specs, check_vma=False
    )
```

profile of v0, /device:TPU:1, one launch (start us, length us, event | category | flops | bytes accessed | tf_op | source)
XLA Modules:
  0.0 820.3 jit_solution(12491529230231990169)
XLA Ops:
  6.6 4.7 copy.41
  11.3 107.9 %while.15 = (s32[]{:T(128)}, f32[256,4096]{1,0:T(8,128)}, s32[32,2]{0,1:T(2,128)S(1)}, f32[32,256,512]{2,1,0:T(8,128)}, s32[]{:T(128)}) while((s32[]{:T(128)}, f32[256,4096]{1,0:T(8,128)}, s32[32,2]{0,1:T(2,128)S(1)}, f32[32,256,512]{2,1,0:T(8,128)}, s32[]{:T(128)}) %tuple.39), condition=%wide.while_cond, body=%wide.while_body.sunk | while | flops 2 | bytes 1049689 | solution.py:14
  62.5 2.8 bitcast_dynamic-update-slice_fusion.2
  65.9 2.8 bitcast_dynamic-update-slice_fusion.2
  69.3 2.8 bitcast_dynamic-update-slice_fusion.2
  120.1 19.3 %fusion.12 = f32[32,256,128]{2,1,0:T(8,128)S(1)} fusion(f32[32,256,512]{2,1,0:T(8,128)} %get-tuple-element.92, f32[32,512,128]{2,1,0:T(8,128)} %param.10), kind=kOutput, calls=%fused_computation.19 | convolution fusion | flops 6442450944 | bytes 29360128 | tf_op jit(solution)/shard_map/sbw,swp->sbp/dot_general | solution.py:17
  139.3 11.5 %fusion.4 = f32[96,256,128]{2,0,1:T(8,128)} fusion(f32[32,256,128]{2,1,0:T(8,128)S(1)} %fusion.12, s32[32]{0:T(128)S(1)} %dynamic-slice_bitcast_fusion), kind=kOutput, calls=%fused_computation.8 | convolution fusion | flops 1207962624 | bytes 16777344 | tf_op jit(solution)/shard_map/rs,sbp->rbp/dot_general | solution.py:25
  150.8 16.4 %copy.16 = f32[96,256,128]{2,1,0:T(8,128)} copy(f32[96,256,128]{2,0,1:T(8,128)} %fusion.4) | data formatting | bytes 25165824 | tf_op jit(solution)/shard_map/rs,sbp->rbp/dot_general | solution.py:25
  167.2 106.7 %reduce-scatter.2.cloned.1.call-done = f32[3,256,128]{2,1,0:T(8,128)} async-done(((f32[96,256,128]{2,1,0:T(8,128)}), f32[3,256,128]{2,1,0:T(8,128)}) %reduce-scatter.2.cloned.1.call-update) | async-done | bytes 393232 | tf_op jit(solution)/shard_map/reduce_scatter | solution.py:26
  276.2 63.9 %all-gather.3.cloned.1.call-done = f32[96,256,128]{2,1,0:T(8,128)} async-done(((f32[3,256,128]{2,1,0:T(8,128)}), f32[96,256,128]{2,1,0:T(8,128)}) %all-gather.3.cloned.1.call-update) | async-done | bytes 12582928 | tf_op jit(solution)/shard_map/all_gather | solution.py:28
  340.1 16.1 %fusion = f32[32,256,128]{2,0,1:T(8,128)S(1)} fusion(f32[96,256,128]{2,1,0:T(8,128)} %all-gather.3.cloned.1.call-done, s32[32]{0:T(128)S(1)} %dynamic-slice_bitcast_fusion), kind=kOutput, calls=%fused_computation.3 | convolution fusion | flops 1207962624 | bytes 16777344 | tf_op jit(solution)/shard_map/rs,rbp->sbp/dot_general | solution.py:29
  356.3 20.9 %fusion.2 = f32[32,256,512]{2,1,0:T(8,128)} fusion(f32[32,512,128]{2,1,0:T(8,128)} %param.10, f32[32,256,128]{2,0,1:T(8,128)S(1)} %fusion), kind=kOutput, calls=%fused_computation.6 | convolution fusion | flops 6442450944 | bytes 29360128 | tf_op jit(solution)/shard_map/sbq,swq->sbw/dot_general | solution.py:30
  377.2 246.7 %while.14 = (s32[]{:T(128)}, f32[256,4096]{1,0:T(8,128)}, s32[32]{0:T(128)S(1)}, f32[32,256,512]{2,1,0:T(8,128)}, s32[]{:T(128)}, /*index=5*/s32[]{:T(128)}, s32[]{:T(128)}) while((s32[]{:T(128)}, f32[256,4096]{1,0:T(8,128)}, s32[32]{0:T(128)S(1)}, f32[32,256,512]{2,1,0:T(8,128)}, s32[]{:T(128)}, /*index=5*/s32[]{:T(128)}, s32[]{:T(128)}) %tuple.52), condition=%wide.region_3.4_spmd, body=%wide.region_2.3_spmd.sunk | while | flops 131077 | bytes 2621575 | solution.py:37
  381.2 3.7 dynamic_update_slice.8
  388.8 3.8 dynamic_update_slice.8
  396.5 3.8 dynamic_update_slice.8
  404.3 3.7 dynamic_update_slice.8
  412.0 3.8 dynamic_update_slice.8
  419.7 3.8 dynamic_update_slice.8
  427.4 3.8 dynamic_update_slice.8
  435.1 3.8 dynamic_update_slice.8
  442.9 3.8 dynamic_update_slice.8
  450.6 3.8 dynamic_update_slice.8
  458.3 3.8 dynamic_update_slice.8
  466.1 3.8 dynamic_update_slice.8
  473.8 3.8 dynamic_update_slice.8
  481.5 3.8 dynamic_update_slice.8
  489.2 3.8 dynamic_update_slice.8
  497.0 3.8 dynamic_update_slice.8
  504.7 3.8 dynamic_update_slice.8
  512.4 3.8 dynamic_update_slice.8
  520.2 3.8 dynamic_update_slice.8
  527.9 3.8 dynamic_update_slice.8
  535.6 3.8 dynamic_update_slice.8
  543.4 3.8 dynamic_update_slice.8
  551.1 3.6 dynamic_update_slice.8
  558.6 3.7 dynamic_update_slice.8
  566.3 3.6 dynamic_update_slice.8
  573.8 3.8 dynamic_update_slice.8
  581.5 3.8 dynamic_update_slice.8
  589.3 3.8 dynamic_update_slice.8
  597.0 3.8 dynamic_update_slice.8
  604.7 3.8 dynamic_update_slice.8
  612.5 3.8 dynamic_update_slice.8
  620.2 3.8 dynamic_update_slice.8
  624.0 153.9 %all-gather.5.cloned.1.call-done = f32[1024,4096]{1,0:T(8,128)} async-done(((f32[256,4096]{1,0:T(8,128)}), f32[1024,4096]{1,0:T(8,128)}) %all-gather.5.cloned.1.call-update) | async-done | bytes 16777232 | tf_op jit(solution)/shard_map/all_gather | solution.py:40
  777.8 30.1 %convolution_bitcast_fusion = f32[256,4096]{0,1:T(8,128)} fusion(f32[1024,4096]{1,0:T(8,128)} %all-gather.5.cloned.1.call-done, f32[256,1024]{1,0:T(8,128)S(1)} %copy-done), kind=kOutput, calls=%fused_computation.5 | convolution fusion | flops 12884901888 | bytes 22020096 | tf_op jit(solution)/shard_map/dot_general | solution.py:38
  807.9 5.6 copy.19
  (179 shorter events, 168.7 us)
Async XLA Ops:
  6.5 771.3 %copy-start = (f32[256,1024]{1,0:T(8,128)S(1)}, f32[256,1024]{1,0:T(8,128)}, u32[]{:S(2)}) copy-start(f32[256,1024]{1,0:T(8,128)} %param.15) | copy-start | bytes 3145732
  6.5 4.8 copy-start.4
  6.5 112.7 %copy-start.2 = (s32[32,32]{1,0:T(8,128)S(1)}, s32[32,32]{1,0:T(8,128)}, u32[]{:S(2)}) copy-start(s32[32,32]{1,0:T(8,128)} %param.12) | copy-start | bytes 12292
  6.5 112.7 %copy-start.3 = (s32[96]{0:T(128)S(1)}, s32[96]{0:T(128)}, u32[]{:S(2)}) copy-start(s32[96]{0:T(128)} %param.13) | copy-start | bytes 1156
  6.5 267.4 %reduce-scatter.2.cloned.1.call-start = ((), (), s32[]{:S(2)}) async-start(), calls=%async_computation.1 | async-start | bytes 12976128 | tf_op jit(solution)/shard_map/reduce_scatter | solution.py:26
  167.2 106.7 %copy-start.1 = (f32[3,128,128]{2,1,0:T(8,128)S(1)}, f32[3,128,128]{2,1,0:T(8,128)}, u32[]{:S(2)}) copy-start(f32[3,128,128]{2,1,0:T(8,128)} %param.14) | copy-start | bytes 589828
  167.2 172.9 %all-gather.3.cloned.1.call-start = ((), (), s32[]{:S(2)}) async-start(), calls=%async_computation.2 | async-start | bytes 12976128 | tf_op jit(solution)/shard_map/all_gather | solution.py:28
  276.2 501.7 %all-gather.5.cloned.1.call-start = ((), (), s32[]{:S(2)}) async-start(), calls=%async_computation.3 | async-start | bytes 20971520 | tf_op jit(solution)/shard_map/all_gather | solution.py:40
Sparse Core Ops, SparseCore 0:
  167.3 106.5 reduce-scatter.1
  276.4 63.6 all-gather.2
  624.1 153.7 all-gather.4
where the time goes:
time: 834 us; the launch traced here: 820 us
  waiting for transfers between devices  324 us (39%)
  local copies, waits for them, and re-layouts  273 us (33%)
  matrix products  100 us (12%)
  loops' own time  61.3 us (7%)
  other arithmetic  47.4 us (6%)
  between operations  13.4 us (2%)
    all_gather x1, waiting for transfers between devices, per_device(): lax.all_gather(corrected, 'band', axis=0, tiled=True)  154 us
    dynamic_update_slice x32, local copies, waits for them, and re-layouts, add_window(): lax.dynamic_update_slice_in_dim(current, previous + updates[slot_index],...  120 us
    gather x96, local copies, waits for them, and re-layouts  108 us
    reduce_scatter x1, waiting for transfers between devices, per_device(): lax.psum_scatter(per_atom, 'dom', scatter_dimension=0, tiled=True)  107 us
    all_gather x1, waiting for transfers between devices, per_device(): all_factors = lax.all_gather(owned_factors, 'dom', axis=0, tiled=True)  63.9 us
    another operation x1, loops' own time, per_device(): corrected = lax.fori_loop(0, slot_count, add_window, orbitals)  61.3 us
    add x32, other arithmetic, add_window(): previous + updates[slot_index]  46.6 us
    dot_general x1, matrix products, per_device(): jnp.dot(rotation, lax.all_gather(corrected, 'band', axis=0, tiled=True),...  30.1 us
  transfers between devices with their start and end apart: 3, of which 3 were waited for; matrix products, arithmetic and copies ran while one was open for 0% of the time, Pallas kernels for 0%

commit v1 on v0

--- a/solution.py
+++ b/solution.py
@@ -7,6 +7,16 @@
 
 
 def per_device(orbitals, projectors, window_start, slot_atom, atom_home, atom_matrices, rotation):
+
+    def process_weights_by_axis(field):
+        placed = lax.all_to_all(
+            jnp.stack([field for _ in range(lax.axis_size("dom"))], axis=0),
+            concat_axis=0,
+            split_axis=0,
+            axis_name="dom",
+        )
+        return jnp.concatenate(placed, axis=0)
+
     own_domain = lax.axis_index("dom")
     slot_count = projectors.shape[0]
     window = projectors.shape[1]
@@ -25,7 +35,7 @@
     per_atom = jnp.einsum("rs,sbp->rbp", home_match, partials, precision=HIGHEST)
     owned_sums = lax.psum_scatter(per_atom, "dom", scatter_dimension=0, tiled=True)
     owned_factors = jnp.einsum("abp,apq->abq", owned_sums, atom_matrices, precision=HIGHEST)
-    all_factors = lax.all_gather(owned_factors, "dom", axis=0, tiled=True)
+    all_factors = process_weights_by_axis(owned_factors)
     slot_factors = jnp.einsum("rs,rbp->sbp", home_match, all_factors, precision=HIGHEST)
     updates = jnp.einsum("sbq,swq->sbw", slot_factors, projectors, precision=HIGHEST)
 

time: 834 us -> 977 us (1.17)
  waiting for transfers between devices: 324 us -> 459 us
    all_to_all x0 -> x1, waiting for transfers between devices: none -> 175 us  [process_weights_by_axis(): lax.all_to_all(jnp.stack([field for _ in range(lax.axis_size('dom'))], ax...]
    all_gather x1 -> x0, waiting for transfers between devices: 63.9 us -> none  [per_device(): all_factors = lax.all_gather(owned_factors, 'dom', axis=0, tiled=True)]
    all_gather x1, waiting for transfers between devices: 154 us -> 177 us  [per_device(): lax.all_gather(corrected, 'band', axis=0, tiled=True)]
where the time goes in v1:
time: 977 us; the launch traced here: 964 us
  waiting for transfers between devices  459 us (47%)
  local copies, waits for them, and re-layouts  278 us (28%)
  matrix products  99.3 us (10%)
  loops' own time  60.2 us (6%)
  other arithmetic  47.4 us (5%)
  between operations  13.7 us (1%)
    all_gather x1, waiting for transfers between devices, per_device(): lax.all_gather(corrected, 'band', axis=0, tiled=True)  177 us
    all_to_all x1, waiting for transfers between devices, process_weights_by_axis(): lax.all_to_all(jnp.stack([field for _ in range(lax.axis_size('dom'))], ax...  175 us
    dynamic_update_slice x32, local copies, waits for them, and re-layouts, add_window(): lax.dynamic_update_slice_in_dim(current, previous + updates[slot_index],...  120 us
    reduce_scatter x1, waiting for transfers between devices, per_device(): lax.psum_scatter(per_atom, 'dom', scatter_dimension=0, tiled=True)  107 us
    gather x96, local copies, waits for them, and re-layouts  106 us
    another operation x1, loops' own time, per_device(): corrected = lax.fori_loop(0, slot_count, add_window, orbitals)  60.2 us
    add x32, other arithmetic, add_window(): previous + updates[slot_index]  46.6 us
    dot_general x1, matrix products, per_device(): jnp.dot(rotation, lax.all_gather(corrected, 'band', axis=0, tiled=True),...  30.1 us
  transfers between devices with their start and end apart: 3, of which 3 were waited for; matrix products, arithmetic and copies ran while one was open for 0% of the time, Pallas kernels for 0%

profile of v1, /device:TPU:1, one launch (start us, length us, event | category | flops | bytes accessed | tf_op | source)
XLA Modules:
  0.0 963.6 jit_solution(8386886533152947112)
XLA Ops:
  6.6 4.7 copy.35
  11.3 106.3 %while.15 = (s32[]{:T(128)}, f32[256,4096]{1,0:T(8,128)}, s32[32,2]{0,1:T(2,128)S(1)}, f32[32,256,512]{2,1,0:T(8,128)}, s32[]{:T(128)}) while((s32[]{:T(128)}, f32[256,4096]{1,0:T(8,128)}, s32[32,2]{0,1:T(2,128)S(1)}, f32[32,256,512]{2,1,0:T(8,128)}, s32[]{:T(128)}) %tuple.39), condition=%wide.while_cond, body=%wide.while_body.sunk | while | flops 2 | bytes 1049689 | solution.py:24
  65.1 2.8 bitcast_dynamic-update-slice_fusion.2
  118.5 19.3 %fusion.12 = f32[32,256,128]{2,1,0:T(8,128)S(1)} fusion(f32[32,256,512]{2,1,0:T(8,128)} %get-tuple-element.92, f32[32,512,128]{2,1,0:T(8,128)} %param.10), kind=kOutput, calls=%fused_computation.19 | convolution fusion | flops 6442450944 | bytes 29360128 | tf_op jit(solution)/shard_map/sbw,swp->sbp/dot_general | solution.py:27
  137.7 11.5 %fusion.4 = f32[96,256,128]{2,0,1:T(8,128)} fusion(f32[32,256,128]{2,1,0:T(8,128)S(1)} %fusion.12, s32[32]{0:T(128)S(1)} %dynamic-slice_bitcast_fusion), kind=kOutput, calls=%fused_computation.8 | convolution fusion | flops 1207962624 | bytes 16777344 | tf_op jit(solution)/shard_map/rs,sbp->rbp/dot_general | solution.py:35
  149.2 16.4 %copy.11 = f32[96,256,128]{2,1,0:T(8,128)} copy(f32[96,256,128]{2,0,1:T(8,128)} %fusion.4) | data formatting | bytes 25165824 | tf_op jit(solution)/shard_map/rs,sbp->rbp/dot_general | solution.py:35
  165.6 106.7 %reduce-scatter.2.cloned.1.call-done = f32[3,256,128]{2,1,0:T(8,128)} async-done(((f32[96,256,128]{2,1,0:T(8,128)}), f32[3,256,128]{2,1,0:T(8,128)}) %reduce-scatter.2.cloned.1.call-update) | async-done | bytes 393232 | tf_op jit(solution)/shard_map/reduce_scatter | solution.py:36
  273.8 6.0 stack.2
  279.9 6.7 all-to-all-start
  286.7 174.6 %all-to-all-done = f32[32,3,256,128]{3,2,1,0:T(8,128)} async-done(((f32[32,3,256,128]{3,2,1,0:T(8,128)}), f32[32,3,256,128]{3,2,1,0:T(8,128)}, u32[]{:S(2)}, u32[]{:S(2)}) %all-to-all-start) | async-done | bytes 12582944 | tf_op jit(solution)/shard_map/all_to_all | solution.py:12
  461.3 16.1 %fusion = f32[32,256,128]{2,0,1:T(8,128)S(1)} fusion(f32[96,256,128]{2,1,0:T(8,128)} %bitcast.5, s32[32]{0:T(128)S(1)} %dynamic-slice_bitcast_fusion), kind=kOutput, calls=%fused_computation.3 | convolution fusion | flops 1207962624 | bytes 16777344 | tf_op jit(solution)/shard_map/rs,rbp->sbp/dot_general | solution.py:39
  477.4 21.0 %fusion.2 = f32[32,256,512]{2,1,0:T(8,128)} fusion(f32[32,512,128]{2,1,0:T(8,128)} %param.10, f32[32,256,128]{2,0,1:T(8,128)S(1)} %fusion), kind=kOutput, calls=%fused_computation.6 | convolution fusion | flops 6442450944 | bytes 29360128 | tf_op jit(solution)/shard_map/sbq,swq->sbw/dot_general | solution.py:40
  498.3 245.3 %while.14 = (s32[]{:T(128)}, f32[256,4096]{1,0:T(8,128)}, s32[32]{0:T(128)S(1)}, f32[32,256,512]{2,1,0:T(8,128)}, s32[]{:T(128)}, /*index=5*/s32[]{:T(128)}, s32[]{:T(128)}) while((s32[]{:T(128)}, f32[256,4096]{1,0:T(8,128)}, s32[32]{0:T(128)S(1)}, f32[32,256,512]{2,1,0:T(8,128)}, s32[]{:T(128)}, /*index=5*/s32[]{:T(128)}, s32[]{:T(128)}) %tuple.50), condition=%wide.region_3.4_spmd, body=%wide.region_2.3_spmd.sunk | while | flops 131077 | bytes 2621575 | solution.py:47
  502.2 3.7 dynamic_update_slice.8
  509.8 3.8 dynamic_update_slice.8
  517.5 3.8 dynamic_update_slice.8
  525.2 3.7 dynamic_update_slice.8
  532.8 3.8 dynamic_update_slice.8
  540.5 3.8 dynamic_update_slice.8
  548.2 3.8 dynamic_update_slice.8
  555.9 3.8 dynamic_update_slice.8
  563.6 3.8 dynamic_update_slice.8
  571.2 3.8 dynamic_update_slice.8
  578.9 3.8 dynamic_update_slice.8
  586.6 3.8 dynamic_update_slice.8
  594.3 3.8 dynamic_update_slice.8
  602.0 3.8 dynamic_update_slice.8
  609.7 3.8 dynamic_update_slice.8
  617.3 3.8 dynamic_update_slice.8
  625.0 3.8 dynamic_update_slice.8
  632.7 3.8 dynamic_update_slice.8
  640.4 3.8 dynamic_update_slice.8
  648.1 3.8 dynamic_update_slice.8
  655.8 3.8 dynamic_update_slice.8
  663.4 3.8 dynamic_update_slice.8
  671.1 3.6 dynamic_update_slice.8
  678.6 3.7 dynamic_update_slice.8
  686.2 3.6 dynamic_update_slice.8
  693.7 3.8 dynamic_update_slice.8
  701.4 3.8 dynamic_update_slice.8
  709.1 3.8 dynamic_update_slice.8
  716.8 3.8 dynamic_update_slice.8
  724.4 3.8 dynamic_update_slice.8
  732.1 3.8 dynamic_update_slice.8
  739.8 3.8 dynamic_update_slice.8
  743.6 177.3 %all-gather.2.cloned.1.call-done = f32[1024,4096]{1,0:T(8,128)} async-done(((f32[256,4096]{1,0:T(8,128)}), f32[1024,4096]{1,0:T(8,128)}) %all-gather.2.cloned.1.call-update) | async-done | bytes 16777232 | tf_op jit(solution)/shard_map/all_gather | solution.py:50
  920.9 30.1 %convolution_bitcast_fusion = f32[256,4096]{0,1:T(8,128)} fusion(f32[1024,4096]{1,0:T(8,128)} %all-gather.2.cloned.1.call-done, f32[256,1024]{1,0:T(8,128)S(1)} %copy-done), kind=kOutput, calls=%fused_computation.5 | convolution fusion | flops 12884901888 | bytes 22020096 | tf_op jit(solution)/shard_map/dot_general | solution.py:48
  951.0 5.6 copy.9
  (179 shorter events, 171.5 us)
Async XLA Ops:
  6.5 914.4 %copy-start = (f32[256,1024]{1,0:T(8,128)S(1)}, f32[256,1024]{1,0:T(8,128)}, u32[]{:S(2)}) copy-start(f32[256,1024]{1,0:T(8,128)} %param.15) | copy-start | bytes 3145732
  6.5 4.8 copy-start.4
  6.5 111.1 %copy-start.2 = (s32[32,32]{1,0:T(8,128)S(1)}, s32[32,32]{1,0:T(8,128)}, u32[]{:S(2)}) copy-start(s32[32,32]{1,0:T(8,128)} %param.12) | copy-start | bytes 12292
  6.5 111.1 %copy-start.3 = (s32[96]{0:T(128)S(1)}, s32[96]{0:T(128)}, u32[]{:S(2)}) copy-start(s32[96]{0:T(128)} %param.13) | copy-start | bytes 1156
  6.5 265.8 %reduce-scatter.2.cloned.1.call-start = ((), (), s32[]{:S(2)}) async-start(), calls=%async_computation.2 | async-start | bytes 12976128 | tf_op jit(solution)/shard_map/reduce_scatter | solution.py:36
  165.6 106.8 %copy-start.1 = (f32[3,128,128]{2,1,0:T(8,128)S(1)}, f32[3,128,128]{2,1,0:T(8,128)}, u32[]{:S(2)}) copy-start(f32[3,128,128]{2,1,0:T(8,128)} %param.14) | copy-start | bytes 589828
  279.9 181.4 %all-to-all-start = ((f32[32,3,256,128]{3,2,1,0:T(8,128)}), f32[32,3,256,128]{3,2,1,0:T(8,128)}, u32[]{:S(2)}, u32[]{:S(2)}) async-start(f32[32,3,256,128]{3,2,1,0:T(8,128)} %stack.2), calls=%async_computation.1 | async-start | bytes 25165824 | tf_op jit(solution)/shard_map/all_to_all | solution.py:12
  286.6 634.3 %all-gather.2.cloned.1.call-start = ((), (), s32[]{:S(2)}) async-start(), calls=%async_computation.3 | async-start | bytes 20971520 | tf_op jit(solution)/shard_map/all_gather | solution.py:50
Sparse Core Ops, SparseCore 0:
  165.7 106.5 reduce-scatter.1
  743.7 177.1 all-gather.1
